TPU v7x, 256 devices: a whole 4x4x8 slice. The times are simulated.
256 devices in a mesh: dp: 4 (over x), expert: 64 (over z, y, core).
Axes of the slice: x: 4, y: 4, z: 8, core: 2. Of those that a mesh axis runs over, the one named last changes fastest.
Arguments:
- tokens: bfloat16 [4096, 3584], P('expert'), may hold values from -6 to 6
- expert_ids: int32 [4096, 8], P('expert'), may hold values from 0 to 63, all different within a row; in each aligned block of 64 rows (0 to 63, 64 to 127, ...) at most 8 rows name the same one
- weight_num: int32 [4096, 8], P('expert'), may hold values from 64 to 1023
- gate_proj: bfloat16 [64, 3584, 2048], P('expert', None, 'dp'), may hold values from -0.09375 to 0.09375
- up_proj: bfloat16 [64, 3584, 2048], P('expert', None, 'dp'), may hold values from -0.09375 to 0.09375
- down_proj: bfloat16 [64, 2048, 3584], P('expert', 'dp'), may hold values from -0.125 to 0.125
Outputs:
- combined: bfloat16 [4096, 3584], P('expert', 'dp')
Inputs may be any that keep to these rules, and one draw needn't show every extreme that they name: `expert_ids`: in the 64 rows of one device no expert is named by more than 8 rows, and some device has an expert named by exactly 8 of its rows.
All inputs are finite; a program needn't handle non-finite values.
Results may differ from a plain program's by a relative error of at most 0.015.
Values may be sent and summed in bfloat16 or wider, within the bound.
A program may use at most 192 MiB of HBM per device.

v0:
```python
import jax
import jax.numpy as jnp
from jax import lax
from jax.sharding import PartitionSpec as P

ROOM = 8


def slot_matrices(ids, num, experts, capacity):
    rows = ids.shape[0]
    slots = experts * capacity
    column = jnp.arange(slots, dtype=jnp.int32)[None, :]
    expert_of = column // capacity
    hits = [ids[:, k : k + 1] == expert_of for k in range(ids.shape[1])]
    named = sum((h.astype(jnp.float32) for h in hits))
    weight = sum((jnp.where(h, num[:, k : k + 1], 0) for k, h in enumerate(hits)))
    earlier = jnp.arange(rows)[:, None] > jnp.arange(rows)[None, :]
    position = jnp.dot(
        earlier.astype(jnp.bfloat16), named.astype(jnp.bfloat16), preferred_element_type=jnp.float32
    )
    here = (named > 0) & (position == (column % capacity).astype(jnp.float32))
    high = jnp.where(here, weight // 32 * 32, 0).astype(jnp.bfloat16)
    low = jnp.where(here, weight % 32, 0).astype(jnp.bfloat16)
    return (here.astype(jnp.bfloat16), high, low)


def local(tokens, expert_ids, weight_num, gate_proj, up_proj, down_proj):
    experts = lax.axis_size("expert")
    parts = lax.axis_size("dp")
    width = tokens.shape[1]
    quarter = width // parts
    slots = experts * ROOM
    here, high, low = slot_matrices(expert_ids, weight_num, experts, ROOM)
    mine = lax.dynamic_slice_in_dim(tokens, lax.axis_index("dp") * quarter, quarter, 1)
    outgoing = lax.dot_general(
        here, mine, (((0,), (0,)), ((), ())), preferred_element_type=jnp.float32
    ).astype(jnp.bfloat16)
    arrived = lax.all_to_all(
        outgoing.reshape(experts, ROOM, quarter), "expert", split_axis=0, concat_axis=0, tiled=True
    ).reshape(slots, quarter)
    rows = lax.all_gather(arrived, "dp", axis=0, tiled=True)
    gate_out, up_out = (0.0, 0.0)
    for q in range(parts):
        block = rows[q * slots : (q + 1) * slots]
        cut = slice(q * quarter, (q + 1) * quarter)
        gate_out += jnp.dot(block, gate_proj[0, cut], preferred_element_type=jnp.float32)
        up_out += jnp.dot(block, up_proj[0, cut], preferred_element_type=jnp.float32)
    hidden = (jax.nn.silu(gate_out) * up_out).astype(jnp.bfloat16)
    partial = jnp.concatenate(
        [
            jnp.dot(
                hidden,
                down_proj[0, :, q * quarter : (q + 1) * quarter],
                preferred_element_type=jnp.float32,
            ).astype(jnp.bfloat16)
            for q in range(parts)
        ],
        axis=0,
    )
    summed = lax.psum_scatter(partial, "dp", scatter_dimension=0, tiled=True)
    returned = lax.all_to_all(
        summed.reshape(experts, ROOM, quarter), "expert", split_axis=0, concat_axis=0, tiled=True
    ).reshape(slots, quarter)
    total = jnp.dot(high, returned, preferred_element_type=jnp.float32)
    total += jnp.dot(low, returned, preferred_element_type=jnp.float32)
    return (total / 1024.0).astype(jnp.bfloat16)


def solution(mesh):
    placed = (
        P("expert", None),
        P("expert", None),
        P("expert", None),
        P("expert", None, "dp"),
        P("expert", None, "dp"),
        P("expert", "dp", None),
    )
    return jax.shard_map(
        local, mesh=mesh, in_specs=placed, out_specs=P("expert", "dp"), check_vma=False
    )
```

profile of v0, /device:TPU:1, one launch (start us, length us, event | category | flops | bytes accessed | tf_op | source)
XLA Modules:
  0.0 203.0 jit_solution(10615380470221626891)
XLA Ops:
  6.5 0.0 copy-start
  6.5 0.0 all-gather.2.cloned.1.call-start
  6.5 1.0 slice_bitcast_fusion.15
  7.5 0.3 fusion.5
  7.9 0.0 copy-done
  7.9 0.5 fusion.1
  8.3 38.4 %all_to_all.10 = bf16[64,8,896]{2,1,0:T(8,128)(2,1)} all-to-all(bf16[64,8,896]{2,1,0:T(8,128)(2,1)S(1)} %fusion.1), channel_id=1, replica_groups=mesh['dp'=4,'expert'=64] {'expert'}, dimensions={0} | all-to-all | bytes 1835008 | tf_op jit(solution)/shard_map/all_to_all | solution.py:38
  46.7 0.0 all-gather.2.cloned.1.call-update
  46.7 0.0 reduce-scatter.2.cloned.1.call-start
  46.8 43.6 %all-gather.2.cloned.1.call-done = bf16[2048,896]{1,0:T(8,128)(2,1)} async-done(((bf16[512,896]{1,0:T(8,128)(2,1)}), bf16[2048,896]{1,0:T(8,128)(2,1)}) %all-gather.2.cloned.1.call-update) | async-done | bytes 3670032 | tf_op jit(solution)/shard_map/all_gather | solution.py:41
  90.4 0.0 copy-start.1
  90.4 0.0 copy-start.2
  90.4 2.3 %fusion.21 = f32[512,512]{1,0:T(8,128)S(1)} fusion(bf16[1,3584,512]{2,1,0:T(8,128)(2,1)} %param.9, bf16[2048,896]{1,0:T(8,128)(2,1)} %all-gather.2.cloned.1.call-done), kind=kOutput, calls=%fused_computation.35 | convolution fusion | flops 469762048 | bytes 2883584 | tf_op jit(solution)/shard_map/dot_general | solution.py:46
  92.7 2.5 %convolution_add_fusion.5 = f32[512,512]{1,0:T(8,128)S(1)} fusion(f32[512,512]{1,0:T(8,128)S(1)} %fusion.21, bf16[1,3584,512]{2,1,0:T(8,128)(2,1)} %param.9, bf16[2048,896]{1,0:T(8,128)(2,1)} %all-gather.2.cloned.1.call-done), kind=kOutput, calls=%fused_computation.12 | convolution fusion | flops 470024192 | bytes 3932160 | tf_op jit(solution)/shard_map/dot_general | solution.py:46
  95.3 0.0 copy-done.1
  95.3 0.0 copy-done.2
  95.3 0.0 copy-start.3
  95.3 0.7 convolution_add_fusion.4
  96.0 0.7 convolution_add_fusion.3
  96.7 0.6 copy-done.3
  97.3 0.7 fusion.16
  98.0 0.7 convolution_add_fusion.2
  98.7 0.7 convolution_add_fusion.1
  99.5 0.0 copy-start.5
  99.5 0.8 fusion.2
  100.3 1.2 copy-done.5
  101.5 0.7 convolution_convert_fusion.1
  102.2 0.7 convolution_convert_fusion.2
  102.9 0.7 convolution_convert_fusion.3
  103.7 0.7 convolution_convert_fusion.4
  104.4 8.7 %pad_maximum_fusion = bf16[2048,896]{1,0:T(8,128)(2,1)} fusion(bf16[512,896]{1,0:T(8,128)(2,1)S(1)} %convolution_convert_fusion.1, bf16[512,896]{1,0:T(8,128)(2,1)S(1)} %convolution_convert_fusion.2, bf16[512,896]{1,0:T(8,128)(2,1)S(1)} %convolution_convert_fusion.3, bf16[512,896]{1,0:T(8,128)(2,1)S(1)} %convolution_convert_fusion.4), kind=kLoop, calls=%fused_computation | loop fusion | flops 14680064 | bytes 7340032 | tf_op jit(solution)/shard_map/concatenate | solution.py:49
  113.1 0.0 copy-start.4
  113.1 0.0 reduce-scatter.2.cloned.1.call-update
  113.1 45.6 %reduce-scatter.2.cloned.1.call-done = bf16[512,896]{1,0:T(8,128)(2,1)} async-done(((bf16[2048,896]{1,0:T(8,128)(2,1)}), bf16[512,896]{1,0:T(8,128)(2,1)}) %reduce-scatter.2.cloned.1.call-update) | async-done | bytes 917520 | tf_op jit(solution)/shard_map/reduce_scatter | solution.py:60
  158.7 10.6 %all-to-all-start.1 = ((bf16[64,8,896]{2,1,0:T(8,128)(2,1)}), bf16[64,8,896]{2,1,0:T(8,128)(2,1)S(1)}, u32[]{:S(2)}, u32[]{:S(2)}) async-start(bf16[64,8,896]{2,1,0:T(8,128)(2,1)} %bitcast.83), calls=%async_computation.2 | async-start | bytes 1835008 | tf_op jit(solution)/shard_map/all_to_all | solution.py:61
  169.3 0.0 copy-done.4
  169.4 25.3 %all-to-all-done.1 = bf16[64,8,896]{2,1,0:T(8,128)(2,1)S(1)} async-done(((bf16[64,8,896]{2,1,0:T(8,128)(2,1)}), bf16[64,8,896]{2,1,0:T(8,128)(2,1)S(1)}, u32[]{:S(2)}, u32[]{:S(2)}) %all-to-all-start.1) | async-done | bytes 917536 | tf_op jit(solution)/shard_map/all_to_all | solution.py:61
  194.6 0.5 fusion.7
  195.1 1.1 fusion.4
  (2 shorter events, 0.0 us)
Async XLA Ops:
  6.5 1.3 copy-start
  6.5 83.9 %all-gather.2.cloned.1.call-start = ((), (), s32[]{:S(2)}) async-start(), calls=%async_computation.3 | async-start | bytes 4587520 | tf_op jit(solution)/shard_map/all_gather | solution.py:41
  46.7 112.0 %reduce-scatter.2.cloned.1.call-start = ((), (), s32[]{:S(2)}) async-start(), calls=%async_computation.4 | async-start | bytes 4587520 | tf_op jit(solution)/shard_map/reduce_scatter | solution.py:60
  90.4 4.9 %copy-start.1 = (bf16[2048,896]{1,0:T(8,128)(2,1)S(1)}, bf16[2048,896]{1,0:T(8,128)(2,1)}, u32[]{:S(2)}) copy-start(bf16[2048,896]{1,0:T(8,128)(2,1)} %all-gather.2.cloned.1.call-done) | copy-start | bytes 11010052
  90.4 4.9 %copy-start.2 = (bf16[1,3584,512]{2,1,0:T(8,128)(2,1)S(1)}, bf16[1,3584,512]{2,1,0:T(8,128)(2,1)}, u32[]{:S(2)}) copy-start(bf16[1,3584,512]{2,1,0:T(8,128)(2,1)} %param.9) | copy-start | bytes 11010052
  95.3 2.0 %copy-start.3 = (bf16[1,3584,512]{2,1,0:T(8,128)(2,1)S(1)}, bf16[1,3584,512]{2,1,0:T(8,128)(2,1)}, u32[]{:S(2)}) copy-start(bf16[1,3584,512]{2,1,0:T(8,128)(2,1)} %param.10) | copy-start | bytes 11010052
  99.5 2.0 %copy-start.5 = (bf16[1,512,3584]{2,1,0:T(8,128)(2,1)S(1)}, bf16[1,512,3584]{2,1,0:T(8,128)(2,1)}, u32[]{:S(2)}) copy-start(bf16[1,512,3584]{2,1,0:T(8,128)(2,1)} %param.11) | copy-start | bytes 11010052
  113.1 56.2 %copy-start.4 = (s32[64,8]{0,1:T(8,128)S(1)}, s32[64,8]{0,1:T(8,128)}, u32[]{:S(2)}) copy-start(s32[64,8]{0,1:T(8,128)} %param.8) | copy-start | bytes 6148
  158.7 35.9 %all-to-all-start.1 = ((bf16[64,8,896]{2,1,0:T(8,128)(2,1)}), bf16[64,8,896]{2,1,0:T(8,128)(2,1)S(1)}, u32[]{:S(2)}, u32[]{:S(2)}) async-start(bf16[64,8,896]{2,1,0:T(8,128)(2,1)} %bitcast.83), calls=%async_computation.2 | async-start | bytes 1835008 | tf_op jit(solution)/shard_map/all_to_all | solution.py:61
Sparse Core Ops, SparseCore 0:
  46.8 43.5 all-gather.1
  113.2 45.3 reduce-scatter.1
where the time goes:
time: 203 us
  waiting for transfers between devices  115 us (57%)
  blocking collectives  38.4 us (19%)
  matrix products  14.4 us (7%)
  between operations  13.6 us (7%)
  starting transfers between devices  10.7 us (5%)
  other arithmetic  8.73 us (4%)
  local copies, waits for them, and re-layouts  2.81 us (1%)
    reduce_scatter x1, waiting for transfers between devices, local(): summed = lax.psum_scatter(partial, 'dp', scatter_dimension=0, tiled=True)  45.6 us
    all_gather x1, waiting for transfers between devices, local(): rows = lax.all_gather(arrived, 'dp', axis=0, tiled=True)  43.6 us
    all_to_all x1, blocking collectives, local(): lax.all_to_all(outgoing.reshape(experts, ROOM, quarter), 'expert', split_...  38.4 us
    all_to_all x1, waiting for transfers between devices, local(): lax.all_to_all(summed.reshape(experts, ROOM, quarter), 'expert', split_ax...  25.3 us
    all_to_all x1, starting transfers between devices, local(): lax.all_to_all(summed.reshape(experts, ROOM, quarter), 'expert', split_ax...  10.6 us
    concatenate x1, other arithmetic, local(): jnp.concatenate([jnp.dot(hidden, down_proj[0, :, q * quarter:(q + 1) * qu...  8.72 us
    dot_general x4, matrix products, local(): jnp.dot(block, gate_proj[0, cut], preferred_element_type=jnp.float32)  6.26 us
  transfers between devices with their start and end apart: 3, of which 3 were waited for; matrix products, arithmetic and copies ran while one was open for 0% of the time, Pallas kernels for 0%

commit v1 on v0

--- a/solution.py
+++ b/solution.py
@@ -38,7 +38,20 @@
     arrived = lax.all_to_all(
         outgoing.reshape(experts, ROOM, quarter), "expert", split_axis=0, concat_axis=0, tiled=True
     ).reshape(slots, quarter)
-    rows = lax.all_gather(arrived, "dp", axis=0, tiled=True)
+    ways, here_2, step = (lax.axis_size("dp"), lax.axis_index("dp"), arrived.shape[0])
+    lengths = [n * ways if d == 0 else n for d, n in enumerate(arrived.shape)]
+    rows = lax.dynamic_update_slice_in_dim(
+        jnp.zeros(lengths, arrived.dtype), arrived, here_2 * step, axis=0
+    )
+    going_up = going_down = arrived
+    for far in range(1, ways // 2 + 1):
+        going_up = lax.ppermute(going_up, "dp", [(d, (d + 1) % ways) for d in range(ways)])
+        rows = lax.dynamic_update_slice_in_dim(rows, going_up, (here_2 - far) % ways * step, axis=0)
+        if 2 * far < ways:
+            going_down = lax.ppermute(going_down, "dp", [(d, (d - 1) % ways) for d in range(ways)])
+            rows = lax.dynamic_update_slice_in_dim(
+                rows, going_down, (here_2 + far) % ways * step, axis=0
+            )
     gate_out, up_out = (0.0, 0.0)
     for q in range(parts):
         block = rows[q * slots : (q + 1) * slots]

time: 203 us -> 196 us (0.966)
  waiting for transfers between devices: 115 us -> 106 us
  matrix products: 14.4 us -> 11 us
  starting transfers between devices: 10.7 us -> 13.4 us
  local copies, waits for them, and re-layouts: 2.81 us -> 4.88 us
    all_gather x1 -> x0, waiting for transfers between devices: 43.6 us -> none  [local(): rows = lax.all_gather(arrived, 'dp', axis=0, tiled=True)]
    ppermute x0 -> x3, waiting for transfers between devices: none -> 37.9 us  [the longest x2 37.9 us: local(): lax.ppermute(going_up, 'dp', [(d, (d + 1) % ways) for d in range(ways)])]
    dot_general x4, matrix products: 6.26 us -> 2.83 us  [local(): jnp.dot(block, gate_proj[0, cut], preferred_element_type=jnp.float32)]
    ppermute x0 -> x3, starting transfers between devices: none -> 2.78 us  [the longest x1 1.47 us: local(): lax.ppermute(going_down, 'dp', [(d, (d - 1) % ways) for d in range(ways)])]
    reduce_scatter x1, waiting for transfers between devices: 45.6 us -> 43.2 us  [local(): summed = lax.psum_scatter(partial, 'dp', scatter_dimension=0, tiled=True)]
  transfers between devices with their start and end apart: 3 -> 5, of which waited for: 3 -> 4; matrix products, arithmetic and copies ran while one was open for 0% -> 1% of each run, Pallas kernels for 0% -> 0%
where the time goes in v1:
time: 196 us
  waiting for transfers between devices  106 us (54%)
  blocking collectives  38.3 us (20%)
  between operations  13.6 us (7%)
  starting transfers between devices  13.4 us (7%)
  matrix products  11 us (6%)
  other arithmetic  8.73 us (4%)
  local copies, waits for them, and re-layouts  4.88 us (2%)
    reduce_scatter x1, waiting for transfers between devices, local(): summed = lax.psum_scatter(partial, 'dp', scatter_dimension=0, tiled=True)  43.2 us
    all_to_all x1, blocking collectives, local(): lax.all_to_all(outgoing.reshape(experts, ROOM, quarter), 'expert', split_...  38.3 us
    ppermute x2, waiting for transfers between devices, local(): lax.ppermute(going_up, 'dp', [(d, (d + 1) % ways) for d in range(ways)])  37.9 us
    all_to_all x1, waiting for transfers between devices, local(): lax.all_to_all(summed.reshape(experts, ROOM, quarter), 'expert', split_ax...  25.3 us
    all_to_all x1, starting transfers between devices, local(): lax.all_to_all(summed.reshape(experts, ROOM, quarter), 'expert', split_ax...  10.6 us
    concatenate x1, other arithmetic, local(): jnp.concatenate([jnp.dot(hidden, down_proj[0, :, q * quarter:(q + 1) * qu...  8.73 us
  transfers between devices with their start and end apart: 5, of which 4 were waited for; matrix products, arithmetic and copies ran while one was open for 1% of the time, Pallas kernels for 0%

profile of v1, /device:TPU:1, one launch (start us, length us, event | category | flops | bytes accessed | tf_op | source)
XLA Modules:
  0.0 196.2 jit_solution(454965008988232089)
XLA Ops:
  6.5 0.0 copy-start
  6.5 0.0 reduce-scatter.2.cloned.1.call-start
  6.5 1.0 slice_bitcast_fusion.15
  7.5 0.3 fusion.7
  7.9 0.0 copy-done
  7.9 0.5 fusion.4
  8.3 38.3 %all_to_all.10 = bf16[64,8,896]{2,1,0:T(8,128)(2,1)S(1)} all-to-all(bf16[64,8,896]{2,1,0:T(8,128)(2,1)S(1)} %fusion.4), channel_id=1, replica_groups=mesh['dp'=4,'expert'=64] {'expert'}, dimensions={0} | all-to-all | bytes 1835008 | tf_op jit(solution)/shard_map/all_to_all | solution.py:38
  46.6 1.2 collective-permute-start
  47.8 1.5 collective-permute-start.1
  49.3 19.1 %collective-permute-done = bf16[512,896]{1,0:T(8,128)(2,1)S(1)} collective-permute-done((bf16[512,896]{1,0:T(8,128)(2,1)S(1)}, bf16[512,896]{1,0:T(8,128)(2,1)S(1)}, u32[]{:S(2)}, u32[]{:S(2)}) %collective-permute-start) | collective-permute-done | bytes 917536 | tf_op jit(solution)/shard_map/ppermute | solution.py:48
  68.4 0.1 collective-permute-start.2
  68.5 0.3 broadcast_in_dim.96
  68.8 0.0 copy-start.1
  68.8 0.1 constant_dynamic-update-slice_fusion.3
  68.9 0.1 constant_dynamic-update-slice_fusion.2
  69.1 0.0 collective-permute-done.1
  69.1 1.5 constant_dynamic-update-slice_fusion.1
  70.6 18.7 %collective-permute-done.2 = bf16[512,896]{1,0:T(8,128)(2,1)S(1)} collective-permute-done((bf16[512,896]{1,0:T(8,128)(2,1)S(1)}, bf16[512,896]{1,0:T(8,128)(2,1)S(1)}, u32[]{:S(2)}, u32[]{:S(2)}) %collective-permute-start.2) | collective-permute-done | bytes 917536 | tf_op jit(solution)/shard_map/ppermute | solution.py:48
  89.3 0.1 constant_dynamic-update-slice_fusion
  89.4 0.0 copy-done.1
  89.4 0.7 fusion.24
  90.1 0.0 copy-start.3
  90.2 0.7 fusion.26
  90.9 0.7 fusion.28
  91.6 0.6 copy-done.3
  92.2 0.7 fusion.15
  92.9 0.7 fusion.17
  93.6 0.7 fusion.19
  94.3 0.7 fusion.3
  95.0 0.0 copy-start.4
  95.0 0.9 multiply_convert_fusion
  96.0 1.1 copy-done.4
  97.1 0.7 convolution_convert_fusion.1
  97.8 0.7 convolution_convert_fusion.2
  98.5 0.7 convolution_convert_fusion.3
  99.2 0.7 convolution_convert_fusion.4
  99.9 8.7 %pad_maximum_fusion = bf16[2048,896]{1,0:T(8,128)(2,1)} fusion(bf16[512,896]{1,0:T(8,128)(2,1)S(1)} %convolution_convert_fusion.1, bf16[512,896]{1,0:T(8,128)(2,1)S(1)} %convolution_convert_fusion.2, bf16[512,896]{1,0:T(8,128)(2,1)S(1)} %convolution_convert_fusion.3, bf16[512,896]{1,0:T(8,128)(2,1)S(1)} %convolution_convert_fusion.4), kind=kLoop, calls=%fused_computation | loop fusion | flops 14680064 | bytes 7340032 | tf_op jit(solution)/shard_map/concatenate | solution.py:62
  108.7 0.0 copy-start.2
  108.7 0.0 reduce-scatter.2.cloned.1.call-update
  108.7 43.2 %reduce-scatter.2.cloned.1.call-done = bf16[512,896]{1,0:T(8,128)(2,1)} async-done(((bf16[2048,896]{1,0:T(8,128)(2,1)}), bf16[512,896]{1,0:T(8,128)(2,1)}) %reduce-scatter.2.cloned.1.call-update) | async-done | bytes 917520 | tf_op jit(solution)/shard_map/reduce_scatter | solution.py:73
  151.8 10.6 %all-to-all-start.1 = ((bf16[64,8,896]{2,1,0:T(8,128)(2,1)}), bf16[64,8,896]{2,1,0:T(8,128)(2,1)S(1)}, u32[]{:S(2)}, u32[]{:S(2)}) async-start(bf16[64,8,896]{2,1,0:T(8,128)(2,1)} %bitcast.87), calls=%async_computation.2 | async-start | bytes 1835008 | tf_op jit(solution)/shard_map/all_to_all | solution.py:74
  162.5 0.0 copy-done.2
  162.5 25.3 %all-to-all-done.1 = bf16[64,8,896]{2,1,0:T(8,128)(2,1)S(1)} async-done(((bf16[64,8,896]{2,1,0:T(8,128)(2,1)}), bf16[64,8,896]{2,1,0:T(8,128)(2,1)S(1)}, u32[]{:S(2)}, u32[]{:S(2)}) %all-to-all-start.1) | async-done | bytes 917536 | tf_op jit(solution)/shard_map/all_to_all | solution.py:74
  187.8 0.5 fusion.9
  188.2 1.1 fusion.6
  (2 shorter events, 0.0 us)
Async XLA Ops:
  6.5 1.3 copy-start
  6.5 145.3 %reduce-scatter.2.cloned.1.call-start = ((), (), s32[]{:S(2)}) async-start(), calls=%async_computation.3 | async-start | bytes 4587520 | tf_op jit(solution)/shard_map/reduce_scatter | solution.py:73
  46.6 21.8 %collective-permute-start = (bf16[512,896]{1,0:T(8,128)(2,1)S(1)}, bf16[512,896]{1,0:T(8,128)(2,1)S(1)}, u32[]{:S(2)}, u32[]{:S(2)}) collective-permute-start(bf16[512,896]{1,0:T(8,128)(2,1)S(1)} %bitcast.85), channel_id=1, source_target_pairs={{0,64},{64,128},{128,192},{192,0},{1,65},{65,129},{129,193},{193,1... | collective-permute-start | bytes 2752520 | tf_op jit(solution)/shard_map/ppermute | solution.py:48
  47.8 21.3 %collective-permute-start.1 = (bf16[512,896]{1,0:T(8,128)(2,1)S(1)}, bf16[512,896]{1,0:T(8,128)(2,1)}, u32[]{:S(2)}, u32[]{:S(2)}) collective-permute-start(bf16[512,896]{1,0:T(8,128)(2,1)S(1)} %bitcast.86), channel_id=1, source_target_pairs={{0,192},{64,0},{128,64},{192,128},{1,193},{65,1},{129,65},{193,129... | collective-permute-start | bytes 2752520 | tf_op jit(solution)/shard_map/ppermute | solution.py:51
  68.4 20.9 %collective-permute-start.2 = (bf16[512,896]{1,0:T(8,128)(2,1)S(1)}, bf16[512,896]{1,0:T(8,128)(2,1)S(1)}, u32[]{:S(2)}, u32[]{:S(2)}) collective-permute-start(bf16[512,896]{1,0:T(8,128)(2,1)S(1)} %collective-permute-done), channel_id=1, source_target_pairs={{0,64},{64,128},{128,192},{192,0},{1,65},{65,129},{129,193},{193,1... | collective-permute-start | bytes 2752520 | tf_op jit(solution)/shard_map/ppermute | solution.py:48
  68.8 20.6 %copy-start.1 = (bf16[1,3584,512]{2,1,0:T(8,128)(2,1)S(1)}, bf16[1,3584,512]{2,1,0:T(8,128)(2,1)}, u32[]{:S(2)}) copy-start(bf16[1,3584,512]{2,1,0:T(8,128)(2,1)} %param.9) | copy-start | bytes 11010052
  90.1 2.0 %copy-start.3 = (bf16[1,3584,512]{2,1,0:T(8,128)(2,1)S(1)}, bf16[1,3584,512]{2,1,0:T(8,128)(2,1)}, u32[]{:S(2)}) copy-start(bf16[1,3584,512]{2,1,0:T(8,128)(2,1)} %param.10) | copy-start | bytes 11010052
  95.0 2.0 %copy-start.4 = (bf16[1,512,3584]{2,1,0:T(8,128)(2,1)S(1)}, bf16[1,512,3584]{2,1,0:T(8,128)(2,1)}, u32[]{:S(2)}) copy-start(bf16[1,512,3584]{2,1,0:T(8,128)(2,1)} %param.11) | copy-start | bytes 11010052
  108.7 53.8 %copy-start.2 = (s32[64,8]{0,1:T(8,128)S(1)}, s32[64,8]{0,1:T(8,128)}, u32[]{:S(2)}) copy-start(s32[64,8]{0,1:T(8,128)} %param.8) | copy-start | bytes 6148
  151.8 35.9 %all-to-all-start.1 = ((bf16[64,8,896]{2,1,0:T(8,128)(2,1)}), bf16[64,8,896]{2,1,0:T(8,128)(2,1)S(1)}, u32[]{:S(2)}, u32[]{:S(2)}) async-start(bf16[64,8,896]{2,1,0:T(8,128)(2,1)} %bitcast.87), calls=%async_computation.2 | async-start | bytes 1835008 | tf_op jit(solution)/shard_map/all_to_all | solution.py:74
Sparse Core Ops, SparseCore 0:
  108.8 42.9 reduce-scatter.1
